TPU v7x, 512 devices: a whole 4x8x8 slice. The times are simulated.
512 devices in a mesh: pts: 32 (over z, x), comp: 16 (over y, core).
Axes of the slice: x: 4, y: 8, z: 8, core: 2. Of those that a mesh axis runs over, the one named last changes fastest.
Arguments:
- points: bfloat16 [65536, 3072], P(('pts', 'comp')), may hold values from -6 to 6
- candidates: int32 [65536, 4], P(('pts', 'comp')), may hold values from 0 to 31, all different within a row; in each aligned block of 128 rows (0 to 127, 128 to 255, ...) at most 32 rows name the same one
- means: bfloat16 [4096, 3072], P('comp'), may hold values from -0.75 to 0.75
- variances: float32 [4096], P('comp'), may hold values from 0.9 to 1.1
- log_weights: float32 [4096], P('comp'), may hold values from -4 to 4
Outputs:
- loglik: float32 [65536], P(('pts', 'comp'))
- new_means: float32 [16, 256, 3072], P('comp', 'pts')
- new_variances: float32 [16, 256], P('comp', 'pts')
- new_log_weights: float32 [16, 256], P('comp', 'pts')
Inputs may be any that keep to these rules, and one draw needn't show every extreme that they name: `candidates`: each row names 4 different blocks. Among the 128 rows of one device, no block is named by more than 32 rows, and some block is named by exactly 32 rows.
All inputs are finite; a program needn't handle non-finite values.
Results may differ from a plain program's by a relative error of at most 0.0065.
Values may be sent and summed in bfloat16 or wider, within the bound.
No kernel may reach another device: no remote copies, remote signals or barrier semaphores. Data moves between devices by JAX's collectives and lax.ppermute only.
A program may use at most 64 MiB of HBM per device.

v0:
```python
import math

import jax
import jax.numpy as jnp
from jax import lax
from jax.sharding import PartitionSpec as P


def on_device(points, candidates, means, variances, log_weights):
    ncomp = lax.axis_size("comp")
    nshare = lax.axis_size("pts")
    rows_here = points.shape[0]
    cands = candidates.shape[1]
    width = points.shape[1]
    owned = means.shape[0]
    block = owned // 2
    nblocks = 2 * ncomp
    slots = 2 * rows_here * cands // nblocks
    flat = candidates.reshape(-1)
    onehot = (flat[:, None] == jnp.arange(nblocks, dtype=jnp.int32)[None, :]).astype(jnp.int32)
    position = jnp.sum((jnp.cumsum(onehot, axis=0) - 1) * onehot, axis=1)
    slot = flat * slots + position
    source_row = jnp.arange(rows_here * cands, dtype=jnp.int32) // cands
    slot_rows = jnp.full((nblocks * slots,), rows_here, jnp.int32).at[slot].set(source_row)
    outgoing = jnp.take(points, slot_rows, axis=0, mode="fill", fill_value=0).reshape(
        ncomp, 2 * slots, width
    )
    arrived = lax.all_to_all(outgoing, "comp", split_axis=0, concat_axis=0, tiled=True).reshape(
        ncomp, 2, slots, width
    )
    mu_blocks = means.reshape(2, block, width)
    inner = jnp.einsum("slcd,lkd->slck", arrived, mu_blocks, preferred_element_type=jnp.float32)
    sq_rows = jnp.einsum("slcd,slcd->slc", arrived, arrived, preferred_element_type=jnp.float32)
    sq_means = jnp.einsum("lkd,lkd->lk", mu_blocks, mu_blocks, preferred_element_type=jnp.float32)
    var_blocks = variances.reshape(2, block)
    const = log_weights.reshape(2, block) - 0.5 * width * jnp.log(2.0 * math.pi * var_blocks)
    logp = const[None, :, None, :] - (
        sq_rows[..., None] - 2.0 * inner + sq_means[None, :, None, :]
    ) / (2.0 * var_blocks[None, :, None, :])
    block_max = jnp.max(logp, axis=3)
    block_sum = jnp.sum(jnp.exp(logp - block_max[..., None]), axis=3)
    back_max, back_sum = (
        lax.all_to_all(
            block_max.reshape(ncomp, 2 * slots), "comp", split_axis=0, concat_axis=0, tiled=True
        ),
        lax.all_to_all(
            block_sum.reshape(ncomp, 2 * slots), "comp", split_axis=0, concat_axis=0, tiled=True
        ),
    )
    pair_max = back_max.reshape(-1)[slot].reshape(rows_here, cands)
    pair_sum = back_sum.reshape(-1)[slot].reshape(rows_here, cands)
    top = jnp.max(pair_max, axis=1)
    loglik = top + jnp.log(jnp.sum(pair_sum * jnp.exp(pair_max - top[:, None]), axis=1))
    slot_totals = jnp.take(loglik, slot_rows, axis=0, mode="fill", fill_value=1e30).reshape(
        ncomp, 2 * slots
    )
    totals = lax.all_to_all(slot_totals, "comp", split_axis=0, concat_axis=0, tiled=True).reshape(
        ncomp, 2, slots
    )
    resp = jnp.exp(logp - totals[..., None])
    counts = jnp.sum(resp, axis=(0, 2)).reshape(owned)
    sqsum = jnp.sum(resp * sq_rows[..., None], axis=(0, 2)).reshape(owned)
    resp_half = resp.astype(jnp.bfloat16)
    wsum = jnp.einsum(
        "slck,slcd->lkd", resp_half, arrived, preferred_element_type=jnp.float32
    ).reshape(owned, width)
    share = owned // nshare
    first_row = lax.axis_index("pts") * share
    wsum_all, counts_all, sqsum_all = lax.psum((wsum, counts, sqsum), "pts")
    wsum_own = lax.dynamic_slice_in_dim(wsum_all, first_row, share, 0)
    counts_own = lax.dynamic_slice_in_dim(counts_all, first_row, share, 0)
    sqsum_own = lax.dynamic_slice_in_dim(sqsum_all, first_row, share, 0)
    mu_old = lax.dynamic_slice_in_dim(means, first_row, share, 0).astype(jnp.float32)
    var_old = lax.dynamic_slice_in_dim(variances, first_row, share, 0)
    new_means = (wsum_own + mu_old) / (counts_own + 1.0)[:, None]
    resid = (
        sqsum_own
        - 2.0 * jnp.sum(new_means * wsum_own, axis=1)
        + counts_own * jnp.sum(new_means * new_means, axis=1)
        + width * var_old
    )
    new_variances = resid / (width * (counts_own + 1.0))
    total_points = rows_here * ncomp * nshare
    new_log_weights = jnp.log((counts_own + 1.0) / float(total_points + owned * ncomp))
    return (
        loglik,
        new_means.reshape(1, share, width),
        new_variances.reshape(1, share),
        new_log_weights.reshape(1, share),
    )


def solution(mesh):
    return jax.shard_map(
        on_device,
        mesh=mesh,
        in_specs=(
            P(("pts", "comp"), None),
            P(("pts", "comp"), None),
            P("comp", None),
            P("comp"),
            P("comp"),
        ),
        out_specs=(P(("pts", "comp")), P("comp", "pts", None), P("comp", "pts"), P("comp", "pts")),
        check_vma=False,
    )
```

profile of v0, /device:TPU:8, one launch (start us, length us, event | category | flops | bytes accessed | tf_op | source)
XLA Modules:
  0.0 411.9 jit_solution(16513333544923814898)
XLA Ops:
  7.2 0.9 copy.27
  8.3 0.7 broadcast_multiply_fusion
  9.0 1.2 reduce-window.6
  10.7 2.4 scatter_custom_fusion
  13.3 6.8 %gather_fusion = bf16[1024,3072]{1,0:T(8,128)(2,1)} fusion(bf16[128,3072]{1,0:T(8,128)(2,1)S(1)} %copy-done, s32[1024]{0:T(1024)S(1)} %fusion.31), kind=kCustom, calls=%fused_computation | custom fusion | bytes 12587008 | tf_op jit(solution)/shard_map/jit(_take)/gather | solution.py:25
  20.1 5.9 %broadcast_select_fusion = bf16[16,64,3072]{2,1,0:T(8,128)(2,1)} fusion(bf16[16,64,3072]{2,1,0:T(8,128)(2,1)} %bitcast.52, pred[16,64]{1,0:T(8,128)(4,1)S(1)} %broadcast_in_dim.35), kind=kLoop, calls=%fused_computation.7 | loop fusion | flops 3145728 | bytes 12583936 | tf_op jit(solution)/shard_map/jit(_take)/select_n | solution.py:25
  26.0 10.3 %all-to-all-start = ((bf16[16,64,3072]{2,1,0:T(8,128)(2,1)}), bf16[16,64,3072]{2,1,0:T(8,128)(2,1)}, u32[]{:S(2)}, u32[]{:S(2)}) async-start(bf16[16,64,3072]{2,1,0:T(8,128)(2,1)} %broadcast_select_fusion), calls=%async_computation | async-start | bytes 12582912 | tf_op jit(solution)/shard_map/all_to_all | solution.py:28
  36.3 0.4 fusion.5
  36.7 136.9 %all-to-all-done = bf16[16,64,3072]{2,1,0:T(8,128)(2,1)} async-done(((bf16[16,64,3072]{2,1,0:T(8,128)(2,1)}), bf16[16,64,3072]{2,1,0:T(8,128)(2,1)}, u32[]{:S(2)}, u32[]{:S(2)}) %all-to-all-start) | async-done | bytes 6291488 | tf_op jit(solution)/shard_map/all_to_all | solution.py:28
  173.6 4.1 fusion
  177.7 4.7 %fusion.38 = (f32[16,2,32]{2,0,1:T(8,128)S(1)}, f32[16,2,32,128]{3,2,0,1:T(8,128)S(1)}) fusion(f32[2,128]{1,0:T(2,128)S(1)} %get-tuple-element.14, f32[2,128]{1,0:T(2,128)S(1)} %fusion.5, bf16[2,128,3072,1]{2,1,3,0:T(8,128)(2,1)S(1)} %bitcast.55, bf16[16,2,32,3072]{3,2,1,0:T(8,128)(2,1)} %bitcast.5, f32[16,2,32]{2,0,1:T(8,128)S(1)} %copy.40, ...), kind=kOutput, calls=%fused_computation.61 | convolution fusion | flops 806091776 | bytes 8399872 | tf_op jit(solution)/shard_map/slcd,lkd->slck/dot_general | solution.py:32
  182.4 0.4 exponential_reduce_fusion
  182.8 0.7 all_to_all.22
  183.5 6.7 %all-to-all-start.2 = ((f32[16,1,64]{2,1,0:T(1,128)}), f32[16,1,64]{2,1,0:T(1,128)S(1)}, u32[]{:S(2)}, u32[]{:S(2)}) async-start(f32[16,1,64]{2,1,0:T(1,128)} %bitcast.12), calls=%async_computation.2 | async-start | bytes 16384 | tf_op jit(solution)/shard_map/all_to_all | solution.py:46
  190.2 0.7 all_to_all.20
  190.9 5.5 %all-to-all-done.2 = f32[16,1,64]{2,1,0:T(1,128)S(1)} async-done(((f32[16,1,64]{2,1,0:T(1,128)}), f32[16,1,64]{2,1,0:T(1,128)S(1)}, u32[]{:S(2)}, u32[]{:S(2)}) %all-to-all-start.2) | async-done | bytes 4128 | tf_op jit(solution)/shard_map/all_to_all | solution.py:46
  196.4 4.7 %all-to-all-start.1 = ((f32[16,1,64]{2,1,0:T(1,128)}), f32[16,1,64]{2,1,0:T(1,128)S(1)}, u32[]{:S(2)}, u32[]{:S(2)}) async-start(f32[16,1,64]{2,1,0:T(1,128)} %bitcast.11), calls=%async_computation.1 | async-start | bytes 16384 | tf_op jit(solution)/shard_map/all_to_all | solution.py:43
  201.2 0.5 broadcast.159
  201.7 0.7 reduce.16
  202.5 2.3 gather_fusion.2
  204.9 2.5 all-to-all-done.1
  207.3 0.7 reduce.15
  208.1 2.3 gather_fusion.1
  210.8 6.6 %gather_fusion.3 = f32[1024]{0:T(1024)S(1)} fusion(f32[128]{0:T(128)S(1)} %log_add_fusion, s32[1024]{0:T(1024)S(1)} %fusion.31), kind=kCustom, calls=%fused_computation.3 | custom fusion | bytes 12288 | tf_op jit(solution)/shard_map/jit(_take)/gather | solution.py:54
  217.5 10.8 %all_to_all.29 = f32[16,1,64]{2,1,0:T(1,128)S(1)} all-to-all(f32[16,1,64]{2,1,0:T(1,128)S(1)} %select_n.56), channel_id=1, replica_groups=mesh['pts'=32,'comp'=16] {'comp'}, dimensions={0} | all-to-all | bytes 8192 | tf_op jit(solution)/shard_map/all_to_all | solution.py:57
  228.3 0.7 reduce.17
  229.1 5.6 %fusion.1 = f32[2,128,3072,1]{2,1,3,0:T(8,128)} fusion(bf16[16,2,32,3072]{3,2,1,0:T(8,128)(2,1)} %bitcast.5, f32[16,2,32,128]{3,2,0,1:T(8,128)S(1)} %get-tuple-element.16, f32[16,2,32]{2,0,1:T(8,128)S(1)} %copy.35), kind=kOutput, calls=%fused_computation.8 | convolution fusion | flops 805568512 | bytes 9965568 | tf_op jit(solution)/shard_map/slck,slcd->lkd/dot_general | solution.py:64
  235.1 78.4 %all-reduce = (f32[256]{0:T(256)S(1)}, f32[256]{0:T(256)S(1)}) all-reduce(f32[256]{0:T(256)S(1)} %bitcast.61, f32[256]{0:T(256)S(1)} %bitcast.60), channel_id=1, replica_groups=mesh['pts'=32,'comp'=16] {'pts'}, use_global_device_ids=true, to_apply=%region_10.11 | all-reduce | flops 512 | bytes 4096 | tf_op jit(solution)/shard_map/psum | solution.py:69
  313.5 0.6 log_bitcast_fusion
  314.1 88.6 %all-reduce.3.cloned.1.call-done = f32[256,3072]{1,0:T(8,128)} async-done(((f32[256,3072]{1,0:T(8,128)}), f32[256,3072]{1,0:T(8,128)}) %all-reduce.3.cloned.1.call-update) | async-done | bytes 3145744 | tf_op jit(solution)/shard_map/psum | solution.py:69
  402.7 1.8 multiply_reduce_fusion.2
  404.5 0.6 fusion.37
  (43 shorter events, 2.2 us)
Async XLA Ops:
  7.2 6.1 %copy-start = (bf16[128,3072]{1,0:T(8,128)(2,1)S(1)}, bf16[128,3072]{1,0:T(8,128)(2,1)}, u32[]{:S(2)}) copy-start(bf16[128,3072]{1,0:T(8,128)(2,1)} %param.5) | copy-start | bytes 2359300
  26.0 10.3 %copy-start.2 = (bf16[256,3072]{1,0:T(8,128)(2,1)S(1)}, bf16[256,3072]{1,0:T(8,128)(2,1)}, u32[]{:S(2)}) copy-start(bf16[256,3072]{1,0:T(8,128)(2,1)} %param.7) | copy-start | bytes 4718596
  26.0 10.7 %copy-start.3 = (f32[256]{0:T(256)S(1)}, f32[256]{0:T(256)}, u32[]{:S(2)}) copy-start(f32[256]{0:T(256)} %param.8) | copy-start | bytes 3076
  26.0 10.7 %copy-start.4 = (f32[256]{0:T(256)S(1)}, f32[256]{0:T(256)}, u32[]{:S(2)}) copy-start(f32[256]{0:T(256)} %param.9) | copy-start | bytes 3076
  26.0 147.6 %all-to-all-start = ((bf16[16,64,3072]{2,1,0:T(8,128)(2,1)}), bf16[16,64,3072]{2,1,0:T(8,128)(2,1)}, u32[]{:S(2)}, u32[]{:S(2)}) async-start(bf16[16,64,3072]{2,1,0:T(8,128)(2,1)} %broadcast_select_fusion), calls=%async_computation | async-start | bytes 12582912 | tf_op jit(solution)/shard_map/all_to_all | solution.py:28
  183.5 13.0 %all-to-all-start.2 = ((f32[16,1,64]{2,1,0:T(1,128)}), f32[16,1,64]{2,1,0:T(1,128)S(1)}, u32[]{:S(2)}, u32[]{:S(2)}) async-start(f32[16,1,64]{2,1,0:T(1,128)} %bitcast.12), calls=%async_computation.2 | async-start | bytes 16384 | tf_op jit(solution)/shard_map/all_to_all | solution.py:46
  196.4 10.9 %all-to-all-start.1 = ((f32[16,1,64]{2,1,0:T(1,128)}), f32[16,1,64]{2,1,0:T(1,128)S(1)}, u32[]{:S(2)}, u32[]{:S(2)}) async-start(f32[16,1,64]{2,1,0:T(1,128)} %bitcast.11), calls=%async_computation.1 | async-start | bytes 16384 | tf_op jit(solution)/shard_map/all_to_all | solution.py:43
  201.2 201.6 %all-reduce.3.cloned.1.call-start = ((), (), s32[]{:S(2)}) async-start(), calls=%async_computation.4 | async-start | bytes 6291456 | tf_op jit(solution)/shard_map/psum | solution.py:69
  210.8 23.9 %copy-start.1 = (f32[128]{0:T(128)}, f32[128]{0:T(128)S(1)}, u32[]{:S(2)}) copy-start(f32[128]{0:T(128)S(1)} %log_add_fusion) | copy-start | bytes 1540
Sparse Core Ops, SparseCore 0:
  234.8 167.8 all-reduce.2
where the time goes:
time: 413 us; the launch traced here: 412 us
  waiting for transfers between devices  234 us (57%)
  blocking collectives  89.2 us (22%)
  local copies, waits for them, and re-layouts  24.4 us (6%)
  starting transfers between devices  21.8 us (5%)
  other arithmetic  18.4 us (4%)
  between operations  14.2 us (3%)
  matrix products  10.3 us (2%)
    all_to_all x1, waiting for transfers between devices, on_device(): lax.all_to_all(outgoing, 'comp', split_axis=0, concat_axis=0, tiled=True)  137 us
    psum x1, waiting for transfers between devices, on_device(): wsum_all, counts_all, sqsum_all = lax.psum((wsum, counts, sqsum), 'pts')  88.6 us
    psum x1, blocking collectives, on_device(): wsum_all, counts_all, sqsum_all = lax.psum((wsum, counts, sqsum), 'pts')  78.4 us
    all_to_all x1, blocking collectives, on_device(): lax.all_to_all(slot_totals, 'comp', split_axis=0, concat_axis=0, tiled=True)  10.8 us
    all_to_all x1, starting transfers between devices, on_device(): lax.all_to_all(outgoing, 'comp', split_axis=0, concat_axis=0, tiled=True)  10.3 us
  transfers between devices with their start and end apart: 4, of which 4 were waited for; matrix products, arithmetic and copies ran while one was open for 1% of the time, Pallas kernels for 0%

commit v1 on v0

v1 whole, which is shorter than its diff:
```python
import math

import jax
import jax.numpy as jnp
from jax import lax
from jax.sharding import PartitionSpec as P

LOW = -1e30


def split3(v):
    hi = lax.reduce_precision(v, 8, 7)
    mid = lax.reduce_precision(v - hi, 8, 7)
    lo = v - hi - mid
    return [hi, mid, lo]


def make_body(npts, ncomp, nx):
    nz = npts // nx
    ny = ncomp // 2
    clockwise = [(c, (c + 2) % ncomp) for c in range(ncomp)]
    counter = [(c, (c - 2) % ncomp) for c in range(ncomp)]
    partner = [(c, c ^ 1) for c in range(ncomp)]
    same_core = [[2 * y + core for y in range(ny)] for core in range(2)]
    along_x = [[z * nx + x for x in range(nx)] for z in range(nz)]
    along_z = [[z * nx + x for z in range(nz)] for x in range(nx)]

    def on_device(points, candidates, means, variances, log_weights):
        rows, width = points.shape
        owned = means.shape[0]
        block = owned // 2
        share = owned // npts
        me = lax.axis_index("comp")
        my_y = me // 2
        f32 = jnp.float32
        bf16 = jnp.bfloat16

        chunks = [None] * ny
        chunks[0] = points
        up = down = points
        for step in range(1, ny // 2):
            up = lax.ppermute(up, "comp", clockwise)
            down = lax.ppermute(down, "comp", counter)
            chunks[step] = up
            chunks[ny - step] = down
        half = rows // 2
        top_half = lax.ppermute(up[:half], "comp", clockwise)
        low_half = lax.ppermute(down[half:], "comp", counter)
        chunks[ny // 2] = jnp.concatenate([top_half, low_half], axis=0)

        def regroup(v):
            tail = v.shape[1:]
            order = (1, 0, 2) + tuple(range(3, 3 + len(tail)))
            return v.reshape((nz, nx, share) + tail).transpose(order).reshape(v.shape)

        my_means = regroup(means)
        their_means = lax.ppermute(my_means, "comp", partner)
        mu = jnp.concatenate([my_means, their_means], axis=0)
        small = jnp.stack([regroup(variances), regroup(log_weights)])
        small = jnp.concatenate([small, lax.ppermute(small, "comp", partner)], axis=1)
        var, logw = small[0], small[1]
        mm = jnp.sum(mu.astype(f32) ** 2, axis=1)
        const = logw - 0.5 * width * jnp.log(2.0 * math.pi * var)
        local_block = regroup(jnp.arange(owned, dtype=jnp.int32) // block)
        block_of = jnp.concatenate([2 * me + local_block, 2 * (me ^ 1) + local_block])

        cand_all = lax.all_to_all(
            jnp.broadcast_to(candidates[None], (ny,) + candidates.shape),
            "comp",
            split_axis=0,
            concat_axis=0,
            axis_index_groups=same_core,
            tiled=True,
        )

        logps, lses, xxs = [], [], []
        for r in range(ny):
            x = chunks[r]
            cand = lax.dynamic_index_in_dim(cand_all, (my_y - r) % ny, 0, keepdims=False)
            inner = lax.dot_general(x, mu, (((1,), (1,)), ((), ())), preferred_element_type=f32)
            xx = jnp.sum(x.astype(f32) ** 2, axis=1)
            logp = const[None, :] - (xx[:, None] - 2.0 * inner + mm[None, :]) / (2.0 * var[None, :])
            named = cand[:, 0:1] == block_of[None, :]
            for i in range(1, candidates.shape[1]):
                named = named | (cand[:, i : i + 1] == block_of[None, :])
            logp = jnp.where(named, logp, LOW)
            top = jnp.max(logp, axis=1)
            lses.append(top + jnp.log(jnp.sum(jnp.exp(logp - top[:, None]), axis=1)))
            logps.append(logp)
            xxs.append(xx)

        lse = jnp.stack(lses)
        source = (my_y - jnp.arange(ny, dtype=jnp.int32)) % ny
        match = source[:, None] == jnp.arange(ny, dtype=jnp.int32)[None, :]
        lse_abs = jnp.sum(jnp.where(match[:, :, None], lse[:, None, :], 0.0), axis=0)
        shared = lax.all_to_all(
            jnp.broadcast_to(lse_abs.reshape(1, ny * rows), (ny, ny * rows)),
            "comp",
            split_axis=0,
            concat_axis=0,
            axis_index_groups=same_core,
            tiled=True,
        )
        peak = jnp.max(shared, axis=0)
        total = (peak + jnp.log(jnp.sum(jnp.exp(shared - peak[None]), axis=0))).reshape(ny, rows)
        total_rel = jnp.sum(jnp.where(match[:, :, None], total[None], 0.0), axis=1)
        loglik = total_rel[0]

        logp = jnp.concatenate(logps, axis=0)
        xx = jnp.concatenate(xxs, axis=0)
        x_all = jnp.concatenate(chunks, axis=0)
        resp = jnp.exp(logp - total_rel.reshape(-1)[:, None])
        counts = jnp.sum(resp, axis=0)
        sqsum = jnp.sum(resp * xx[:, None], axis=0)
        resp16 = resp.astype(bf16)

        def summed(part):
            return lax.dot_general(part, x_all, (((0,), (0,)), ((), ())), preferred_element_type=f32)

        def packed(w, c, s):
            extra = jnp.stack(split3(c) + split3(s), axis=1)
            extra = jnp.pad(extra, ((0, 0), (0, 128 - extra.shape[1])))
            return jnp.concatenate([w.astype(bf16), extra.astype(bf16)], axis=1)

        def unpacked(total):
            w = total[:, :width]
            c = total[:, width] + total[:, width + 1] + total[:, width + 2]
            s = total[:, width + 3] + total[:, width + 4] + total[:, width + 5]
            return w, c, s

        theirs = packed(summed(resp16[:, owned:]), counts[owned:], sqsum[owned:])
        from_partner = lax.ppermute(theirs, "comp", partner)
        mine = summed(resp16[:, :owned])
        w, c, s = unpacked(from_partner.astype(f32))
        out = packed(mine + w, counts[:owned] + c, sqsum[:owned] + s)

        got = lax.all_to_all(
            out, "pts", split_axis=0, concat_axis=0, axis_index_groups=along_x, tiled=True
        ).reshape(nx, owned // nx, width + 128)
        w, c, s = unpacked(jnp.sum(got.astype(f32), axis=0))
        got = lax.all_to_all(
            packed(w, c, s), "pts", split_axis=0, concat_axis=0, axis_index_groups=along_z, tiled=True
        ).reshape(nz, share, width + 128)
        wsum_own, counts_own, sqsum_own = unpacked(jnp.sum(got.astype(f32), axis=0))

        first_row = lax.axis_index("pts") * share
        mu_old = lax.dynamic_slice_in_dim(means, first_row, share, 0).astype(f32)
        var_old = lax.dynamic_slice_in_dim(variances, first_row, share, 0)
        new_means = (wsum_own + mu_old) / (counts_own + 1.0)[:, None]
        resid = (
            sqsum_own
            - 2.0 * jnp.sum(new_means * wsum_own, axis=1)
            + counts_own * jnp.sum(new_means * new_means, axis=1)
            + width * var_old
        )
        new_variances = resid / (width * (counts_own + 1.0))
        total_points = rows * ncomp * npts
        new_log_weights = jnp.log((counts_own + 1.0) / float(total_points + owned * ncomp))
        return (
            loglik,
            new_means.reshape(1, share, width),
            new_variances.reshape(1, share),
            new_log_weights.reshape(1, share),
        )

    return on_device


def solution(mesh):
    return jax.shard_map(
        make_body(mesh.shape["pts"], mesh.shape["comp"], 4),
        mesh=mesh,
        in_specs=(
            P(("pts", "comp"), None),
            P(("pts", "comp"), None),
            P("comp", None),
            P("comp"),
            P("comp"),
        ),
        out_specs=(P(("pts", "comp")), P("comp", "pts", None), P("comp", "pts"), P("comp", "pts")),
        check_vma=False,
    )
```

time: 413 us -> 182 us (0.44)
  the two profiles are of different devices: /device:TPU:8 before, /device:TPU:2 now
where the time goes in v1:
time: 182 us; the launch traced here: 181 us
  starting transfers between devices  56.1 us (31%)
  waiting for transfers between devices  35.5 us (20%)
  matrix products  26.5 us (15%)
  blocking collectives  26 us (14%)
  other arithmetic  20.2 us (11%)
  local copies, waits for them, and re-layouts  15.1 us (8%)
    all_to_all x1, blocking collectives, on_device(): lax.all_to_all(out, 'pts', split_axis=0, concat_axis=0, axis_index_groups...  26 us
    dot_general x8, matrix products, on_device(): lax.dot_general(x, mu, (((1,), (1,)), ((), ())), preferred_element_type=f32)  19 us
    all_to_all x1, waiting for transfers between devices, on_device(): lax.all_to_all(packed(w, c, s), 'pts', split_axis=0, concat_axis=0, axis_...  13.7 us
    ppermute x3, starting transfers between devices, on_device(): up = lax.ppermute(up, 'comp', clockwise)  12.4 us
    all_to_all x1, starting transfers between devices, on_device(): lax.all_to_all(packed(w, c, s), 'pts', split_axis=0, concat_axis=0, axis_...  9.22 us
    ppermute x3, starting transfers between devices, on_device(): down = lax.ppermute(down, 'comp', counter)  9.13 us
    unnamed x34, local copies, waits for them, and re-layouts  9 us
    dot_general x2, matrix products, summed(): lax.dot_general(part, x_all, (((0,), (0,)), ((), ())), preferred_element_...  7.54 us
  transfers between devices with their start and end apart: 14, of which 7 were waited for; matrix products, arithmetic and copies ran while one was open for 21% of the time, Pallas kernels for 0%

profile of v1, /device:TPU:2, one launch (start us, length us, event | category | flops | bytes accessed | tf_op | source)
XLA Modules:
  0.0 181.0 jit_solution(16786058796692574872)
XLA Ops:
  0.7 3.6 %collective-permute-start.2 = (bf16[128,3072]{1,0:T(8,128)(2,1)}, bf16[128,3072]{1,0:T(8,128)(2,1)}, u32[]{:S(2)}, u32[]{:S(2)}) collective-permute-start(bf16[128,3072]{1,0:T(8,128)(2,1)} %param.5), channel_id=1, source_target_pairs={{0,2},{1,3},{2,4},{3,5},{4,6},{5,7},{6,8},{7,9},{8,10},{9,11},{10,... | collective-permute-start | bytes 2359304 | tf_op jit(solution)/shard_map/ppermute | solution.py:42
  4.3 3.8 %collective-permute-start.6 = (bf16[128,3072]{1,0:T(8,128)(2,1)}, bf16[128,3072]{1,0:T(8,128)(2,1)S(1)}, u32[]{:S(2)}, u32[]{:S(2)}) collective-permute-start(bf16[128,3072]{1,0:T(8,128)(2,1)} %param.5), channel_id=1, source_target_pairs={{0,14},{1,15},{2,0},{3,1},{4,2},{5,3},{6,4},{7,5},{8,6},{9,7},{10,... | collective-permute-start | bytes 2359304 | tf_op jit(solution)/shard_map/ppermute | solution.py:43
  9.4 6.9 %all-to-all-start = ((s32[8,128,4]{1,2,0:T(4,128)}), s32[8,128,4]{1,2,0:T(4,128)S(1)}, u32[]{:S(2)}, u32[]{:S(2)}) async-start(s32[8,128,4]{1,2,0:T(4,128)} %broadcast_in_dim.40), calls=%async_computation | async-start | bytes 32768 | tf_op jit(solution)/shard_map/all_to_all | solution.py:67
  20.1 2.4 %collective-permute-start = (f32[2,256]{1,0:T(2,128)S(1)}, f32[2,256]{1,0:T(2,128)S(1)}, u32[]{:S(2)}, u32[]{:S(2)}) collective-permute-start(f32[2,256]{1,0:T(2,128)S(1)} %pad_maximum_fusion.2), channel_id=1, source_target_pairs={{0,1},{1,0},{2,3},{3,2},{4,5},{5,4},{6,7},{7,6},{8,9},{9,8},{10,11... | collective-permute-start | bytes 6152 | tf_op jit(solution)/shard_map/ppermute | solution.py:60
  24.2 4.4 %all-to-all-done = s32[8,128,4]{1,2,0:T(4,128)S(1)} async-done(((s32[8,128,4]{1,2,0:T(4,128)}), s32[8,128,4]{1,2,0:T(4,128)S(1)}, u32[]{:S(2)}, u32[]{:S(2)}) %all-to-all-start) | async-done | bytes 16416 | tf_op jit(solution)/shard_map/all_to_all | solution.py:67
  28.8 5.0 %collective-permute-start.3 = (bf16[128,3072]{1,0:T(8,128)(2,1)}, bf16[128,3072]{1,0:T(8,128)(2,1)S(1)}, u32[]{:S(2)}, u32[]{:S(2)}) collective-permute-start(bf16[128,3072]{1,0:T(8,128)(2,1)} %collective-permute-done.2), channel_id=1, source_target_pairs={{0,2},{1,3},{2,4},{3,5},{4,6},{5,7},{6,8},{7,9},{8,10},{9,11},{10,... | collective-permute-start | bytes 2359304 | tf_op jit(solution)/shard_map/ppermute | solution.py:42
  37.5 2.1 %constant_dynamic-update-slice_fusion.17 = bf16[1024,3072]{1,0:T(8,128)(2,1)} fusion(bf16[1024,3072]{1,0:T(8,128)(2,1)} %constant_dynamic-update-slice_fusion.18, bf16[128,3072]{1,0:T(8,128)(2,1)} %collective-permute-done.2), kind=kLoop, calls=%fused_computation.86 | loop fusion | bytes 1572864
  39.6 2.1 %multiply_reduce_fusion = f32[512]{0:T(512)S(1)} fusion(bf16[256,3072]{1,0:T(8,128)(2,1)} %collective-permute-done.1, bf16[256,3072]{1,0:T(8,128)(2,1)S(1)} %bitcast.151), kind=kLoop, calls=%fused_computation | loop fusion | flops 9436672 | bytes 3147776 | tf_op jit(solution)/shard_map/reduce_sum | solution.py:62
  41.7 2.3 %fusion.40 = (f32[128]{0:T(128)S(1)}, f32[128,512]{0,1:T(8,128)S(1)}) fusion(f32[512]{0:T(512)S(1)} %bitcast.166, f32[512]{0:T(512)S(1)} %multiply_reduce_fusion, bf16[128,3072]{1,0:T(8,128)(2,1)S(1)} %copy-done, bf16[256,3072]{1,0:T(8,128)(2,1)} %collective-permute-done.1, bf16[256,3072]{1,0:T(8,128)(2,1)S(1)} %bitcast.152, ...), kind=kOutput, calls=%fused_computation.220 | convolution fusion | flops 409862016 | bytes 4205568 | tf_op jit(solution)/shard_map/dot_general | solution.py:80
  44.8 2.8 %fusion.41 = (f32[128]{0:T(128)S(1)}, f32[128,512]{0,1:T(8,128)S(1)}) fusion(f32[512]{0:T(512)S(1)} %bitcast.167, f32[512]{0:T(512)S(1)} %multiply_reduce_fusion, bf16[128,3072]{1,0:T(8,128)(2,1)} %collective-permute-done.2, bf16[256,3072]{1,0:T(8,128)(2,1)} %collective-permute-done.1, bf16[256,3072]{1,0:T(8,128)(2,1)S(1)} %bitcast.153, ...), kind=kOutput, calls=%fused_computation.221 | convolution fusion | flops 409862016 | bytes 4205568 | tf_op jit(solution)/shard_map/dot_general | solution.py:80
  50.2 3.8 %collective-permute-start.4 = (bf16[128,3072]{1,0:T(8,128)(2,1)S(1)}, bf16[128,3072]{1,0:T(8,128)(2,1)S(1)}, u32[]{:S(2)}, u32[]{:S(2)}) collective-permute-start(bf16[128,3072]{1,0:T(8,128)(2,1)S(1)} %collective-permute-done.3), channel_id=1, source_target_pairs={{0,2},{1,3},{2,4},{3,5},{4,6},{5,7},{6,8},{7,9},{8,10},{9,11},{10,... | collective-permute-start | bytes 2359304 | tf_op jit(solution)/shard_map/ppermute | solution.py:42
  54.2 2.3 %fusion.42 = (f32[128]{0:T(128)S(1)}, f32[128,512]{0,1:T(8,128)S(1)}) fusion(f32[512]{0:T(512)S(1)} %bitcast.168, f32[512]{0:T(512)S(1)} %multiply_reduce_fusion, bf16[128,3072]{1,0:T(8,128)(2,1)S(1)} %collective-permute-done.3, bf16[256,3072]{1,0:T(8,128)(2,1)} %collective-permute-done.1, bf16[256,3072]{1,0:T(8,128)(2,1)S(1)} %bitcast.154, ...), kind=kOutput, calls=%fused_computation.222 | convolution fusion | flops 409862016 | bytes 4205568 | tf_op jit(solution)/shard_map/dot_general | solution.py:80
  57.3 3.3 %collective-permute-start.8 = (bf16[128,3072]{1,0:T(8,128)(2,1)S(1)}, bf16[128,3072]{1,0:T(8,128)(2,1)S(1)}, u32[]{:S(2)}, u32[]{:S(2)}) collective-permute-start(bf16[128,3072]{1,0:T(8,128)(2,1)S(1)} %collective-permute-done.7), channel_id=1, source_target_pairs={{0,14},{1,15},{2,0},{3,1},{4,2},{5,3},{6,4},{7,5},{8,6},{9,7},{10,... | collective-permute-start | bytes 2359304 | tf_op jit(solution)/shard_map/ppermute | solution.py:43
  60.8 2.3 %fusion.46 = (f32[128]{0:T(128)S(1)}, f32[128,512]{0,1:T(8,128)S(1)}) fusion(f32[512]{0:T(512)S(1)} %bitcast.169, f32[512]{0:T(512)S(1)} %multiply_reduce_fusion, bf16[128,3072]{1,0:T(8,128)(2,1)S(1)} %collective-permute-done.7, bf16[256,3072]{1,0:T(8,128)(2,1)} %collective-permute-done.1, bf16[256,3072]{1,0:T(8,128)(2,1)S(1)} %bitcast.155, ...), kind=kOutput, calls=%fused_computation.226 | convolution fusion | flops 409862016 | bytes 4205568 | tf_op jit(solution)/shard_map/dot_general | solution.py:80
  63.1 2.3 %fusion.47 = (f32[128]{0:T(128)S(1)}, f32[128,512]{0,1:T(8,128)S(1)}) fusion(f32[512]{0:T(512)S(1)} %bitcast.170, f32[512]{0:T(512)S(1)} %multiply_reduce_fusion, bf16[128,3072]{1,0:T(8,128)(2,1)S(1)} %collective-permute-done.6, bf16[256,3072]{1,0:T(8,128)(2,1)} %collective-permute-done.1, bf16[256,3072]{1,0:T(8,128)(2,1)S(1)} %bitcast.156, ...), kind=kOutput, calls=%fused_computation.227 | convolution fusion | flops 409862016 | bytes 4205568 | tf_op jit(solution)/shard_map/dot_general | solution.py:80
  66.4 4.1 %collective-permute-done.4 = bf16[128,3072]{1,0:T(8,128)(2,1)S(1)} collective-permute-done((bf16[128,3072]{1,0:T(8,128)(2,1)S(1)}, bf16[128,3072]{1,0:T(8,128)(2,1)S(1)}, u32[]{:S(2)}, u32[]{:S(2)}) %collective-permute-start.4) | collective-permute-done | bytes 786464 | tf_op jit(solution)/shard_map/ppermute | solution.py:42
  70.5 2.5 %collective-permute-start.5 = (bf16[64,3072]{1,0:T(8,128)(2,1)S(1)}, bf16[64,3072]{1,0:T(8,128)(2,1)S(1)}, u32[]{:S(2)}, u32[]{:S(2)}) collective-permute-start(bf16[64,3072]{1,0:T(8,128)(2,1)S(1)} %slice.259), channel_id=1, source_target_pairs={{0,2},{1,3},{2,4},{3,5},{4,6},{5,7},{6,8},{7,9},{8,10},{9,11},{10,... | collective-permute-start | bytes 1179656 | tf_op jit(solution)/shard_map/ppermute | solution.py:47
  73.0 3.0 %collective-permute-done.8 = bf16[128,3072]{1,0:T(8,128)(2,1)S(1)} collective-permute-done((bf16[128,3072]{1,0:T(8,128)(2,1)S(1)}, bf16[128,3072]{1,0:T(8,128)(2,1)S(1)}, u32[]{:S(2)}, u32[]{:S(2)}) %collective-permute-start.8) | collective-permute-done | bytes 786464 | tf_op jit(solution)/shard_map/ppermute | solution.py:43
  76.1 4.7 %collective-permute-start.9 = (bf16[64,3072]{1,0:T(8,128)(2,1)S(1)}, bf16[64,3072]{1,0:T(8,128)(2,1)S(1)}, u32[]{:S(2)}, u32[]{:S(2)}) collective-permute-start(bf16[64,3072]{1,0:T(8,128)(2,1)S(1)} %slice.260), channel_id=1, source_target_pairs={{0,14},{1,15},{2,0},{3,1},{4,2},{5,3},{6,4},{7,5},{8,6},{9,7},{10,... | collective-permute-start | bytes 1179656 | tf_op jit(solution)/shard_map/ppermute | solution.py:48
  82.2 2.3 %fusion.43 = (f32[128]{0:T(128)S(1)}, f32[128,512]{0,1:T(8,128)S(1)}) fusion(f32[512]{0:T(512)S(1)} %bitcast.171, f32[512]{0:T(512)S(1)} %multiply_reduce_fusion, bf16[128,3072]{1,0:T(8,128)(2,1)S(1)} %collective-permute-done.4, bf16[256,3072]{1,0:T(8,128)(2,1)} %collective-permute-done.1, bf16[256,3072]{1,0:T(8,128)(2,1)S(1)} %bitcast.157, ...), kind=kOutput, calls=%fused_computation.223 | convolution fusion | flops 409862016 | bytes 4205568 | tf_op jit(solution)/shard_map/dot_general | solution.py:80
  84.5 2.3 %fusion.45 = (f32[128]{0:T(128)S(1)}, f32[128,512]{0,1:T(8,128)S(1)}) fusion(f32[512]{0:T(512)S(1)} %bitcast.172, f32[512]{0:T(512)S(1)} %multiply_reduce_fusion, bf16[128,3072]{1,0:T(8,128)(2,1)S(1)} %collective-permute-done.8, bf16[256,3072]{1,0:T(8,128)(2,1)} %collective-permute-done.1, bf16[256,3072]{1,0:T(8,128)(2,1)S(1)} %bitcast.158, ...), kind=kOutput, calls=%fused_computation.225 | convolution fusion | flops 409862016 | bytes 4205568 | tf_op jit(solution)/shard_map/dot_general | solution.py:80
  89.5 2.3 %fusion.44 = (f32[128]{0:T(128)S(1)}, f32[128,512]{0,1:T(8,128)S(1)}) fusion(f32[512]{0:T(512)S(1)} %bitcast.173, f32[512]{0:T(512)S(1)} %multiply_reduce_fusion, bf16[128,3072]{1,0:T(8,128)(2,1)S(1)} %get-tuple-element.28, bf16[256,3072]{1,0:T(8,128)(2,1)} %collective-permute-done.1, bf16[256,3072]{1,0:T(8,128)(2,1)S(1)} %bitcast.159, ...), kind=kOutput, calls=%fused_computation.224 | convolution fusion | flops 409862016 | bytes 4205568 | tf_op jit(solution)/shard_map/dot_general | solution.py:80
  95.6 4.6 %all-to-all-start.1 = ((f32[8,1,1024]{2,1,0:T(1,128)}), f32[8,1,1024]{2,1,0:T(1,128)S(1)}, u32[]{:S(2)}, u32[]{:S(2)}) async-start(f32[8,1,1024]{2,1,0:T(1,128)} %broadcast_in_dim.45), calls=%async_computation.1 | async-start | bytes 65536 | tf_op jit(solution)/shard_map/all_to_all | solution.py:96
  103.1 5.1 %all-to-all-done.1 = f32[8,1,1024]{2,1,0:T(1,128)S(1)} async-done(((f32[8,1,1024]{2,1,0:T(1,128)}), f32[8,1,1024]{2,1,0:T(1,128)S(1)}, u32[]{:S(2)}, u32[]{:S(2)}) %all-to-all-start.1) | async-done | bytes 32800 | tf_op jit(solution)/shard_map/all_to_all | solution.py:96
  108.4 2.1 %multiply_reduce_fusion.1 = (f32[512]{0:T(512)S(1)}, f32[512]{0:T(512)S(1)}, bf16[1024,512]{0,1:T(8,128)(2,1)S(1)}) fusion(f32[1024,512]{0,1:T(8,128)} %get-tuple-element.31, f32[1024]{0:T(1024)S(1)} %constant_dynamic-update-slice_fusion.20, f32[1024]{0:T(1024)S(1)} %bitcast.164), kind=kLoop, calls=%fused_computation.9 | loop fusion | flops 2620416 | bytes 3158016 | tf_op jit(solution)/shard_map/reduce_sum | solution.py:114
  110.8 4.6 %convolution_convert_fusion = bf16[256,3072]{1,0:T(8,128)(2,1)S(1)} fusion(bf16[1024,3072]{1,0:T(8,128)(2,1)} %constant_dynamic-update-slice_fusion.10, bf16[1024,512]{0,1:T(8,128)(2,1)S(1)} %get-tuple-element.20), kind=kOutput, calls=%fused_computation.2 | convolution fusion | flops 1611399168 | bytes 8388608 | tf_op jit(solution)/shard_map/dot_general | solution.py:118
  115.6 2.3 %collective-permute-start.10 = (bf16[256,3200]{1,0:T(8,128)(2,1)S(1)}, bf16[256,3200]{1,0:T(8,128)(2,1)S(1)}, u32[]{:S(2)}, u32[]{:S(2)}) collective-permute-start(bf16[256,3200]{1,0:T(8,128)(2,1)S(1)} %fusion.3), channel_id=1, source_target_pairs={{0,1},{1,0},{2,3},{3,2},{4,5},{5,4},{6,7},{7,6},{8,9},{9,8},{10,11... | collective-permute-start | bytes 4915208 | tf_op jit(solution)/shard_map/ppermute | solution.py:132
  117.9 3.3 %collective-permute-done.10 = bf16[256,3200]{1,0:T(8,128)(2,1)S(1)} collective-permute-done((bf16[256,3200]{1,0:T(8,128)(2,1)S(1)}, bf16[256,3200]{1,0:T(8,128)(2,1)S(1)}, u32[]{:S(2)}, u32[]{:S(2)}) %collective-permute-start.10) | collective-permute-done | bytes 1638432 | tf_op jit(solution)/shard_map/ppermute | solution.py:132
  121.4 3.0 %fusion = bf16[256,3072]{1,0:T(8,128)(2,1)} fusion(bf16[1024,3072]{1,0:T(8,128)(2,1)S(1)} %copy-done.3, f32[256,3200]{1,0:T(8,128)S(1)} %convert_element_type.68, bf16[1024,512]{0,1:T(8,128)(2,1)S(1)} %get-tuple-element.20), kind=kOutput, calls=%fused_computation.3 | convolution fusion | flops 1612185600 | bytes 11534336 | tf_op jit(solution)/shard_map/dot_general | solution.py:118
  126.6 26.0 %all_to_all.32 = bf16[4,64,3200]{2,1,0:T(8,128)(2,1)S(1)} all-to-all(bf16[4,64,3200]{2,1,0:T(8,128)(2,1)S(1)} %bitcast.149), channel_id=1, replica_groups={{0,16,32,48},{64,80,96,112},{128,144,160,176},{192,208,224,240},{256,27..., dimensions={0} | all-to-all | bytes 3276800 | tf_op jit(solution)/shard_map/all_to_all | solution.py:137
  154.4 9.2 %all-to-all-start.3 = ((bf16[8,8,3200]{2,1,0:T(8,128)(2,1)}), bf16[8,8,3200]{2,1,0:T(8,128)(2,1)S(1)}, u32[]{:S(2)}, u32[]{:S(2)}) async-start(bf16[8,8,3200]{2,1,0:T(8,128)(2,1)} %fusion.17), calls=%async_computation.3 | async-start | bytes 819200 | tf_op jit(solution)/shard_map/all_to_all | solution.py:141
  164.1 13.7 %all-to-all-done.3 = bf16[8,8,3200]{2,1,0:T(8,128)(2,1)S(1)} async-done(((bf16[8,8,3200]{2,1,0:T(8,128)(2,1)}), bf16[8,8,3200]{2,1,0:T(8,128)(2,1)S(1)}, u32[]{:S(2)}, u32[]{:S(2)}) %all-to-all-start.3) | async-done | bytes 409632 | tf_op jit(solution)/shard_map/all_to_all | solution.py:141
  (141 shorter events, 34.8 us)
Async XLA Ops:
  0.6 22.1 %copy-start = (bf16[128,3072]{1,0:T(8,128)(2,1)S(1)}, bf16[128,3072]{1,0:T(8,128)(2,1)}, u32[]{:S(2)}) copy-start(bf16[128,3072]{1,0:T(8,128)(2,1)} %param.5) | copy-start | bytes 2359300
  0.6 19.1 %copy-start.4 = (f32[256]{0:T(256)S(1)}, f32[256]{0:T(256)}, u32[]{:S(2)}) copy-start(f32[256]{0:T(256)} %param.8) | copy-start | bytes 3076
  0.7 19.3 %copy-start.5 = (f32[256]{0:T(256)S(1)}, f32[256]{0:T(256)}, u32[]{:S(2)}) copy-start(f32[256]{0:T(256)} %param.9) | copy-start | bytes 3076
  0.7 28.1 %collective-permute-start.2 = (bf16[128,3072]{1,0:T(8,128)(2,1)}, bf16[128,3072]{1,0:T(8,128)(2,1)}, u32[]{:S(2)}, u32[]{:S(2)}) collective-permute-start(bf16[128,3072]{1,0:T(8,128)(2,1)} %param.5), channel_id=1, source_target_pairs={{0,2},{1,3},{2,4},{3,5},{4,6},{5,7},{6,8},{7,9},{8,10},{9,11},{10,... | collective-permute-start | bytes 2359304 | tf_op jit(solution)/shard_map/ppermute | solution.py:42
  4.3 29.5 %collective-permute-start.6 = (bf16[128,3072]{1,0:T(8,128)(2,1)}, bf16[128,3072]{1,0:T(8,128)(2,1)S(1)}, u32[]{:S(2)}, u32[]{:S(2)}) collective-permute-start(bf16[128,3072]{1,0:T(8,128)(2,1)} %param.5), channel_id=1, source_target_pairs={{0,14},{1,15},{2,0},{3,1},{4,2},{5,3},{6,4},{7,5},{8,6},{9,7},{10,... | collective-permute-start | bytes 2359304 | tf_op jit(solution)/shard_map/ppermute | solution.py:43
  9.4 19.3 %all-to-all-start = ((s32[8,128,4]{1,2,0:T(4,128)}), s32[8,128,4]{1,2,0:T(4,128)S(1)}, u32[]{:S(2)}, u32[]{:S(2)}) async-start(s32[8,128,4]{1,2,0:T(4,128)} %broadcast_in_dim.40), calls=%async_computation | async-start | bytes 32768 | tf_op jit(solution)/shard_map/all_to_all | solution.py:67
  17.8 21.8 %collective-permute-start.1 = (bf16[256,3072]{1,0:T(8,128)(2,1)S(1)}, bf16[256,3072]{1,0:T(8,128)(2,1)}, u32[]{:S(2)}, u32[]{:S(2)}) collective-permute-start(bf16[256,3072]{1,0:T(8,128)(2,1)S(1)} %bitcast.150), channel_id=1, source_target_pairs={{0,1},{1,0},{2,3},{3,2},{4,5},{5,4},{6,7},{7,6},{8,9},{9,8},{10,11... | collective-permute-start | bytes 4718600 | tf_op jit(solution)/shard_map/ppermute | solution.py:57
  20.1 4.0 %collective-permute-start = (f32[2,256]{1,0:T(2,128)S(1)}, f32[2,256]{1,0:T(2,128)S(1)}, u32[]{:S(2)}, u32[]{:S(2)}) collective-permute-start(f32[2,256]{1,0:T(2,128)S(1)} %pad_maximum_fusion.2), channel_id=1, source_target_pairs={{0,1},{1,0},{2,3},{3,2},{4,5},{5,4},{6,7},{7,6},{8,9},{9,8},{10,11... | collective-permute-start | bytes 6152 | tf_op jit(solution)/shard_map/ppermute | solution.py:60
  28.8 21.4 %collective-permute-start.3 = (bf16[128,3072]{1,0:T(8,128)(2,1)}, bf16[128,3072]{1,0:T(8,128)(2,1)S(1)}, u32[]{:S(2)}, u32[]{:S(2)}) collective-permute-start(bf16[128,3072]{1,0:T(8,128)(2,1)} %collective-permute-done.2), channel_id=1, source_target_pairs={{0,2},{1,3},{2,4},{3,5},{4,6},{5,7},{6,8},{7,9},{8,10},{9,11},{10,... | collective-permute-start | bytes 2359304 | tf_op jit(solution)/shard_map/ppermute | solution.py:42
  33.8 23.4 %collective-permute-start.7 = (bf16[128,3072]{1,0:T(8,128)(2,1)S(1)}, bf16[128,3072]{1,0:T(8,128)(2,1)S(1)}, u32[]{:S(2)}, u32[]{:S(2)}) collective-permute-start(bf16[128,3072]{1,0:T(8,128)(2,1)S(1)} %collective-permute-done.6), channel_id=1, source_target_pairs={{0,14},{1,15},{2,0},{3,1},{4,2},{5,3},{6,4},{7,5},{8,6},{9,7},{10,... | collective-permute-start | bytes 2359304 | tf_op jit(solution)/shard_map/ppermute | solution.py:43
  50.2 20.3 %collective-permute-start.4 = (bf16[128,3072]{1,0:T(8,128)(2,1)S(1)}, bf16[128,3072]{1,0:T(8,128)(2,1)S(1)}, u32[]{:S(2)}, u32[]{:S(2)}) collective-permute-start(bf16[128,3072]{1,0:T(8,128)(2,1)S(1)} %collective-permute-done.3), channel_id=1, source_target_pairs={{0,2},{1,3},{2,4},{3,5},{4,6},{5,7},{6,8},{7,9},{8,10},{9,11},{10,... | collective-permute-start | bytes 2359304 | tf_op jit(solution)/shard_map/ppermute | solution.py:42
  57.3 5.8 %copy-start.1 = (bf16[128,3072]{1,0:T(8,128)(2,1)}, bf16[128,3072]{1,0:T(8,128)(2,1)S(1)}, u32[]{:S(2)}) copy-start(bf16[128,3072]{1,0:T(8,128)(2,1)S(1)} %collective-permute-done.7) | copy-start | bytes 2359300
  57.3 18.8 %collective-permute-start.8 = (bf16[128,3072]{1,0:T(8,128)(2,1)S(1)}, bf16[128,3072]{1,0:T(8,128)(2,1)S(1)}, u32[]{:S(2)}, u32[]{:S(2)}) collective-permute-start(bf16[128,3072]{1,0:T(8,128)(2,1)S(1)} %collective-permute-done.7), channel_id=1, source_target_pairs={{0,14},{1,15},{2,0},{3,1},{4,2},{5,3},{6,4},{7,5},{8,6},{9,7},{10,... | collective-permute-start | bytes 2359304 | tf_op jit(solution)/shard_map/ppermute | solution.py:43
  70.5 17.1 %collective-permute-start.5 = (bf16[64,3072]{1,0:T(8,128)(2,1)S(1)}, bf16[64,3072]{1,0:T(8,128)(2,1)S(1)}, u32[]{:S(2)}, u32[]{:S(2)}) collective-permute-start(bf16[64,3072]{1,0:T(8,128)(2,1)S(1)} %slice.259), channel_id=1, source_target_pairs={{0,2},{1,3},{2,4},{3,5},{4,6},{5,7},{6,8},{7,9},{8,10},{9,11},{10,... | collective-permute-start | bytes 1179656 | tf_op jit(solution)/shard_map/ppermute | solution.py:47
  76.1 12.3 %collective-permute-start.9 = (bf16[64,3072]{1,0:T(8,128)(2,1)S(1)}, bf16[64,3072]{1,0:T(8,128)(2,1)S(1)}, u32[]{:S(2)}, u32[]{:S(2)}) collective-permute-start(bf16[64,3072]{1,0:T(8,128)(2,1)S(1)} %slice.260), channel_id=1, source_target_pairs={{0,14},{1,15},{2,0},{3,1},{4,2},{5,3},{6,4},{7,5},{8,6},{9,7},{10,... | collective-permute-start | bytes 1179656 | tf_op jit(solution)/shard_map/ppermute | solution.py:48
  91.8 9.4 %copy-start.2 = (bf16[128,3072]{1,0:T(8,128)(2,1)S(1)}, bf16[128,3072]{1,0:T(8,128)(2,1)}, u32[]{:S(2)}) copy-start(bf16[128,3072]{1,0:T(8,128)(2,1)} %copy-done.1) | copy-start | bytes 2359300
  95.6 12.6 %all-to-all-start.1 = ((f32[8,1,1024]{2,1,0:T(1,128)}), f32[8,1,1024]{2,1,0:T(1,128)S(1)}, u32[]{:S(2)}, u32[]{:S(2)}) async-start(f32[8,1,1024]{2,1,0:T(1,128)} %broadcast_in_dim.45), calls=%async_computation.1 | async-start | bytes 65536 | tf_op jit(solution)/shard_map/all_to_all | solution.py:96
  115.4 6.0 %copy-start.3 = (bf16[1024,3072]{1,0:T(8,128)(2,1)S(1)}, bf16[1024,3072]{1,0:T(8,128)(2,1)}, u32[]{:S(2)}) copy-start(bf16[1024,3072]{1,0:T(8,128)(2,1)} %constant_dynamic-update-slice_fusion.10) | copy-start | bytes 18874372
  115.6 5.7 %collective-permute-start.10 = (bf16[256,3200]{1,0:T(8,128)(2,1)S(1)}, bf16[256,3200]{1,0:T(8,128)(2,1)S(1)}, u32[]{:S(2)}, u32[]{:S(2)}) collective-permute-start(bf16[256,3200]{1,0:T(8,128)(2,1)S(1)} %fusion.3), channel_id=1, source_target_pairs={{0,1},{1,0},{2,3},{3,2},{4,5},{5,4},{6,7},{7,6},{8,9},{9,8},{10,11... | collective-permute-start | bytes 4915208 | tf_op jit(solution)/shard_map/ppermute | solution.py:132
  154.4 23.4 %all-to-all-start.3 = ((bf16[8,8,3200]{2,1,0:T(8,128)(2,1)}), bf16[8,8,3200]{2,1,0:T(8,128)(2,1)S(1)}, u32[]{:S(2)}, u32[]{:S(2)}) async-start(bf16[8,8,3200]{2,1,0:T(8,128)(2,1)} %fusion.17), calls=%async_computation.3 | async-start | bytes 819200 | tf_op jit(solution)/shard_map/all_to_all | solution.py:141
